TPU v7x, 128 devices: a whole 4x4x4 slice. The times are simulated.
128 devices in a mesh: lang: 8 (over z, y_lo), fsdp: 16 (over y_hi, x, core).
Axes of the slice: x: 4, y: 4 (y_hi: 2, y_lo: 2; y = y_hi * 2 + y_lo), z: 4, core: 2. Of those that a mesh axis runs over, the one named last changes fastest.
Arguments:
- tokens: bfloat16 [8, 768, 8192], P('lang', 'fsdp'), may hold values from -6 to 6
- grad_out: bfloat16 [8, 768, 8192], P('lang', 'fsdp'), may hold values from -24 to 24
- doc_ids: int32 [8, 768], P('lang'), may hold values from 0 to 95, never falling along the last dimension, each value on 1 to 64 neighbouring positions
- w_gate: bfloat16 [8192, 4096], P(None, 'fsdp'), may hold values from -0.0625 to 0.0625
- w_up: bfloat16 [8192, 4096], P(None, 'fsdp'), may hold values from -0.0625 to 0.0625
- w_down: bfloat16 [4096, 8192], P('fsdp'), may hold values from -0.09375 to 0.09375
Outputs:
- grad_tokens: bfloat16 [8, 768, 8192], P('lang', 'fsdp')
- grad_gate: bfloat16 [8192, 4096], P('lang', 'fsdp')
- grad_up: bfloat16 [8192, 4096], P('lang', 'fsdp')
- grad_down: bfloat16 [4096, 8192], P('fsdp', 'lang')
Inputs may be any that keep to these rules, and one draw needn't show every extreme that they name: `doc_ids`: document numbers never fall along a group's pack.
All inputs are finite; a program needn't handle non-finite values.
Results may differ from a plain program's by a relative error of at most 0.015.
Values may be sent and summed in bfloat16 or wider, within the bound.
No kernel may reach another device: no remote copies, remote signals or barrier semaphores. Data moves between devices by JAX's collectives and lax.ppermute only.
A program may use at most 192 MiB of HBM per device.

v0:
```python
import jax
import jax.numpy as jnp
from jax import lax
from jax.sharding import PartitionSpec as P

epsilon = 1e-06


def sent_together(arrays, axis, dim, along):
    both = jnp.concatenate(arrays, axis=along)
    filled, at, gathered = (lax.all_gather(both, axis, axis=dim, tiled=True), 0, [])
    for a in arrays:
        gathered.append(lax.slice_in_dim(filled, at, at + a.shape[along], axis=along))
        at += a.shape[along]
    return tuple(gathered)


def copy_for_each(value, axis):
    length = lax.axis_size(axis)
    return lax.all_to_all(
        jnp.broadcast_to(value[None], (length, *value.shape)), axis, 0, 0, tiled=True
    )


def taken_together(value, axis):
    return copy_for_each(value, axis).sum(axis=0)


def contract_rows(left, right):
    return lax.dot_general(
        left, right, (((0,), (0,)), ((), ())), preferred_element_type=jnp.float32
    )


def contract_cols(left, right):
    return lax.dot_general(
        left, right, (((1,), (1,)), ((), ())), preferred_element_type=jnp.float32
    )


def body(tokens, grad_out, doc_ids, w_gate, w_up, w_down):
    features, upstream = sent_together((tokens, grad_out), "fsdp", 1, 0)
    features = features[0]
    upstream = upstream[0]
    segment = doc_ids[0]
    width = features.shape[1]
    counts = jnp.sum((segment[:, None] == segment[None, :]).astype(jnp.float32), axis=1)
    inverse = 1.0 / counts
    gate_pre = jnp.dot(features, w_gate, preferred_element_type=jnp.float32)
    up_pre = jnp.dot(features, w_up, preferred_element_type=jnp.float32)
    gate_sig = jax.nn.sigmoid(gate_pre)
    activated = gate_pre * gate_sig
    hidden = (activated * up_pre * inverse[:, None]).astype(jnp.bfloat16)
    hid_grad = contract_cols(upstream, w_down) * inverse[:, None]
    gate_grad = (hid_grad * up_pre * gate_sig * (1.0 + gate_pre * (1.0 - gate_sig))).astype(
        jnp.bfloat16
    )
    up_grad = (hid_grad * activated).astype(jnp.bfloat16)
    stacked = jnp.stack(
        [
            contract_rows(features, gate_grad),
            contract_rows(features, up_grad),
            contract_rows(upstream, hidden),
        ]
    )
    moment = jnp.sum(stacked * stacked, axis=(0, 1)) / (3.0 * width) + epsilon
    ratios = 1.0 / moment
    summed_ratio = taken_together(ratios, "lang")
    weighted = stacked * (ratios / summed_ratio)[None, None, :]
    pieces = lax.all_to_all(
        weighted.astype(jnp.bfloat16)[None], "lang", split_axis=2, concat_axis=0, tiled=True
    )
    shares = jnp.sum(pieces, axis=0, dtype=jnp.float32)
    grad_gate = shares[0].astype(jnp.bfloat16)
    grad_up = shares[1].astype(jnp.bfloat16)
    grad_down = shares[2].T.astype(jnp.bfloat16)
    summed = lax.psum_scatter(
        (contract_cols(gate_grad, w_gate) + contract_cols(up_grad, w_up)).astype(jnp.bfloat16),
        "fsdp",
        scatter_dimension=0,
        tiled=True,
    )
    grad_tokens = summed[None]
    return (grad_tokens, grad_gate, grad_up, grad_down)


def solution(mesh):
    return jax.shard_map(
        body,
        mesh=mesh,
        in_specs=(
            P("lang", "fsdp", None),
            P("lang", "fsdp", None),
            P("lang", None),
            P(None, "fsdp"),
            P(None, "fsdp"),
            P("fsdp", None),
        ),
        out_specs=(
            P("lang", "fsdp", None),
            P("lang", "fsdp"),
            P("lang", "fsdp"),
            P("fsdp", "lang"),
        ),
        check_vma=False,
    )
```

profile of v0, /device:TPU:0, one launch (start us, length us, event | category | flops | bytes accessed | tf_op | source)
XLA Modules:
  0.0 516.3 jit_solution(6174130623956002040)
XLA Ops:
  7.2 0.0 all-gather.2.cloned.1.call-start
  7.2 2.7 pad_maximum_fusion
  10.0 0.0 all-gather.2.cloned.1.call-update
  10.0 0.0 reduce-scatter.2.cloned.1.call-start
  10.0 0.7 reduce.5
  10.7 0.4 convert_reduce_fusion
  11.1 150.3 %all-gather.2.cloned.1.call-done = bf16[2,768,8192]{2,1,0:T(8,128)(2,1)} async-done(((bf16[2,48,8192]{2,1,0:T(8,128)(2,1)}), bf16[2,768,8192]{2,1,0:T(8,128)(2,1)}) %all-gather.2.cloned.1.call-update) | async-done | bytes 25165840 | tf_op jit(solution)/shard_map/all_gather | solution.py:11
  161.4 0.0 copy-start.3
  161.4 7.8 %fusion.6 = f32[768,256]{1,0:T(8,128)S(1)} fusion(bf16[8192,256]{1,0:T(8,128)(2,1)} %param.9, bf16[2,768,8192]{2,1,0:T(8,128)(2,1)} %all-gather.2.cloned.1.call-done), kind=kOutput, calls=%fused_computation.11 | convolution fusion | flops 3221225472 | bytes 17563648 | tf_op jit(solution)/shard_map/dot_general | solution.py:49
  169.2 0.0 copy-done.3
  169.2 0.0 copy-start.4
  169.2 6.6 %fusion.7 = f32[768,256]{1,0:T(8,128)S(1)} fusion(bf16[8192,256]{1,0:T(8,128)(2,1)S(1)} %copy-done.3, bf16[2,768,8192]{2,1,0:T(8,128)(2,1)} %all-gather.2.cloned.1.call-done), kind=kOutput, calls=%fused_computation.12 | convolution fusion | flops 3221225472 | bytes 17563648 | tf_op jit(solution)/shard_map/dot_general | solution.py:50
  175.7 0.0 copy-done.4
  175.8 0.0 copy-start.2
  175.8 8.4 %multiply_convert_fusion.1 = (bf16[768,256]{1,0:T(8,128)(2,1)S(1)}, bf16[768,256]{1,0:T(8,128)(2,1)S(1)}) fusion(f32[768,256]{1,0:T(8,128)S(1)} %fusion.6, f32[768,256]{1,0:T(8,128)S(1)} %fusion.7, f32[768]{0:T(1024)S(1)} %broadcast_divide_fusion, bf16[256,8192]{1,0:T(8,128)(2,1)S(1)} %copy-done.4, bf16[2,768,8192]{2,1,0:T(8,128)(2,1)} %all-gather.2.cloned.1.call-done), kind=kOutput, calls=%fused_computation.17 | convolution fusion | flops 3223977984 | bytes 19139584 | tf_op jit(solution)/shard_map/dot_general | solution.py:36
  184.2 0.0 copy-done.2
  184.2 10.0 %fusion.15 = f32[768,8192]{1,0:T(8,128)} fusion(bf16[768,256]{1,0:T(8,128)(2,1)S(1)} %get-tuple-element.32, bf16[8192,256]{1,0:T(8,128)(2,1)S(1)} %copy-done.2), kind=kOutput, calls=%fused_computation.30 | convolution fusion | flops 3221225472 | bytes 29753344 | tf_op jit(solution)/shard_map/dot_general | solution.py:36
  194.2 15.6 %add_convert_fusion = bf16[768,8192]{1,0:T(8,128)(2,1)} fusion(f32[768,8192]{1,0:T(8,128)} %fusion.15, bf16[768,256]{1,0:T(8,128)(2,1)S(1)} %get-tuple-element.31, bf16[8192,256]{1,0:T(8,128)(2,1)} %param.10), kind=kOutput, calls=%fused_computation.4 | convolution fusion | flops 3233808384 | bytes 42336256 | tf_op jit(solution)/shard_map/dot_general | solution.py:36
  209.8 0.0 reduce-scatter.2.cloned.1.call-update
  209.8 6.7 %fusion.4 = f32[8192,256]{1,0:T(8,128)S(1)} fusion(bf16[768,256]{1,0:T(8,128)(2,1)S(1)} %get-tuple-element.31, bf16[2,768,8192]{2,1,0:T(8,128)(2,1)} %all-gather.2.cloned.1.call-done), kind=kOutput, calls=%fused_computation.9 | convolution fusion | flops 3221225472 | bytes 21364736 | tf_op jit(solution)/shard_map/dot_general | solution.py:30
  216.5 0.0 copy-start
  216.5 11.2 %fusion.5 = f32[8192,256]{1,0:T(8,128)S(1)} fusion(bf16[768,256]{1,0:T(8,128)(2,1)S(1)} %get-tuple-element.32, bf16[2,768,8192]{2,1,0:T(8,128)(2,1)} %all-gather.2.cloned.1.call-done), kind=kOutput, calls=%fused_computation.10 | convolution fusion | flops 3221225472 | bytes 21364736 | tf_op jit(solution)/shard_map/dot_general | solution.py:30
  227.7 0.0 copy-start.1
  227.7 15.7 %fusion.2 = f32[8192,256]{1,0:T(8,128)} fusion(bf16[2,768,8192]{2,1,0:T(8,128)(2,1)} %all-gather.2.cloned.1.call-done, f32[768,256]{1,0:T(8,128)S(1)} %fusion.7, f32[768]{0:T(1024)S(1)} %broadcast_divide_fusion, f32[768,256]{1,0:T(8,128)S(1)} %fusion.6), kind=kOutput, calls=%fused_computation.7 | convolution fusion | flops 3222601728 | bytes 22547456 | tf_op jit(solution)/shard_map/dot_general | solution.py:30
  243.4 0.0 copy-done
  243.4 0.0 copy-done.1
  243.4 8.9 %fusion.1 = f32[256]{0:T(256)S(1)} fusion(f32[1,8192,256]{2,1,0:T(8,128)} %bitcast.44, f32[1,8192,256]{2,1,0:T(8,128)S(1)} %bitcast.40, f32[1,8192,256]{2,1,0:T(8,128)S(1)} %bitcast.42), kind=kLoop, calls=%fused_computation.3 | loop fusion | flops 25165568 | bytes 25166848 | tf_op jit(solution)/shard_map/reduce_sum | solution.py:66
  252.4 10.7 %all_to_all.15 = f32[8,1,256]{2,1,0:T(1,128)S(1)} all-to-all(f32[8,1,256]{2,1,0:T(1,128)S(1)} %broadcast_in_dim.5), channel_id=1, replica_groups=mesh['lang'=8,'fsdp'=16] {'lang'}, dimensions={0} | all-to-all | bytes 16384 | tf_op jit(solution)/shard_map/all_to_all | solution.py:20
  263.1 13.7 %fusion = bf16[1,3,8192,256]{3,2,1,0:T(8,128)(2,1)} fusion(f32[1,1,8192,256]{3,2,1,0:T(8,128)} %bitcast.45, f32[1,1,8192,256]{3,2,1,0:T(8,128)} %bitcast.41, f32[1,1,8192,256]{3,2,1,0:T(8,128)} %bitcast.43, f32[256]{0:T(256)S(1)} %multiply_divide_fusion), kind=kLoop, calls=%fused_computation.1 | loop fusion | flops 25165824 | bytes 37749760 | tf_op jit(solution)/shard_map/convert_element_type | solution.py:71
  276.7 17.9 %copy.20 = bf16[1,3,8192,256]{3,1,0,2:T(4,128)(2,1)S(1)} copy(bf16[1,3,8192,256]{3,2,1,0:T(8,128)(2,1)} %fusion) | data formatting | bytes 25165824 | tf_op jit(solution)/shard_map/convert_element_type | solution.py:71
  294.6 196.0 %all_to_all.16 = bf16[1,3,8192,256]{3,1,0,2:T(4,128)(2,1)} all-to-all(bf16[1,3,8192,256]{3,1,0,2:T(4,128)(2,1)S(1)} %copy.20), channel_id=1, replica_groups=mesh['lang'=8,'fsdp'=16] {'lang'}, dimensions={2} | all-to-all | bytes 25165824 | tf_op jit(solution)/shard_map/all_to_all | solution.py:70
  490.6 9.7 %reduce.4 = bf16[3,1024,256]{2,0,1:T(4,128)(2,1)S(1)} reduce(bf16[3,8,1024,256]{3,0,2,1:T(4,128)(2,1)} %bitcast.39, bf16[]{:T(256)} %constant.14), dimensions={1}, to_apply=%region_4.0.clone | reduce | flops 5505024 | bytes 14155778 | tf_op jit(solution)/shard_map/reduce_sum | solution.py:73
  500.3 3.3 fusion.14
  503.6 3.5 copy.26
  507.1 2.4 copy_bitcast_fusion
  509.4 0.0 reduce-scatter.2.cloned.1.call-done
  (5 shorter events, 0.1 us)
Async XLA Ops:
  7.2 154.2 %all-gather.2.cloned.1.call-start = ((), (), s32[]{:S(2)}) async-start(), calls=%async_computation.3 | async-start | bytes 26738688 | tf_op jit(solution)/shard_map/all_gather | solution.py:11
  10.0 499.5 %reduce-scatter.2.cloned.1.call-start = ((), (), s32[]{:S(2)}) async-start(), calls=%async_computation.4 | async-start | bytes 13369344 | tf_op jit(solution)/shard_map/reduce_scatter | solution.py:77
  161.4 7.8 %copy-start.3 = (bf16[8192,256]{1,0:T(8,128)(2,1)S(1)}, bf16[8192,256]{1,0:T(8,128)(2,1)}, u32[]{:S(2)}) copy-start(bf16[8192,256]{1,0:T(8,128)(2,1)} %param.10) | copy-start | bytes 12582916
  169.2 6.6 %copy-start.4 = (bf16[256,8192]{1,0:T(8,128)(2,1)S(1)}, bf16[256,8192]{1,0:T(8,128)(2,1)}, u32[]{:S(2)}) copy-start(bf16[256,8192]{1,0:T(8,128)(2,1)} %param.11) | copy-start | bytes 12582916
  175.8 8.4 %copy-start.2 = (bf16[8192,256]{1,0:T(8,128)(2,1)S(1)}, bf16[8192,256]{1,0:T(8,128)(2,1)}, u32[]{:S(2)}) copy-start(bf16[8192,256]{1,0:T(8,128)(2,1)} %param.9) | copy-start | bytes 12582916
  216.5 26.9 %copy-start = (f32[8192,256]{1,0:T(8,128)}, f32[8192,256]{1,0:T(8,128)S(1)}, u32[]{:S(2)}) copy-start(f32[8192,256]{1,0:T(8,128)S(1)} %fusion.4) | copy-start | bytes 25165828
  227.7 15.7 %copy-start.1 = (f32[8192,256]{1,0:T(8,128)}, f32[8192,256]{1,0:T(8,128)S(1)}, u32[]{:S(2)}) copy-start(f32[8192,256]{1,0:T(8,128)S(1)} %fusion.5) | copy-start | bytes 25165828
Sparse Core Ops, SparseCore 0:
  10.4 150.9 all-gather.1
  210.0 128.4 reduce-scatter.1
where the time goes:
time: 517 us; the launch traced here: 516 us
  blocking collectives  207 us (40%)
  waiting for transfers between devices  150 us (29%)
  matrix products  81.9 us (16%)
  other arithmetic  36.2 us (7%)
  local copies, waits for them, and re-layouts  27 us (5%)
  between operations  14.2 us (3%)
    all_to_all x1, blocking collectives, body(): lax.all_to_all(weighted.astype(jnp.bfloat16)[None], 'lang', split_axis=2,...  196 us
    all_gather x1, waiting for transfers between devices, sent_together(): lax.all_gather(both, axis, axis=dim, tiled=True)  150 us
    dot_general x3, matrix products, contract_cols(): lax.dot_general(left, right, (((1,), (1,)), ((), ())), preferred_element_...  34 us
    dot_general x3, matrix products, contract_rows(): lax.dot_general(left, right, (((0,), (0,)), ((), ())), preferred_element_...  33.5 us
    convert_element_type x1, local copies, waits for them, and re-layouts, body(): weighted.astype(jnp.bfloat16)[None]  17.9 us
    convert_element_type x1, other arithmetic, body(): weighted.astype(jnp.bfloat16)[None]  13.7 us
    all_to_all x1, blocking collectives, copy_for_each(): lax.all_to_all(jnp.broadcast_to(value[None], (length, *value.shape)), axi...  10.7 us
  transfers between devices with their start and end apart: 2, of which 1 were waited for; matrix products, arithmetic and copies ran while one was open for 18% of the time, Pallas kernels for 0%

commit v1 on v0

--- a/solution.py
+++ b/solution.py
@@ -67,9 +67,10 @@
     ratios = 1.0 / moment
     summed_ratio = taken_together(ratios, "lang")
     weighted = stacked * (ratios / summed_ratio)[None, None, :]
-    pieces = lax.all_to_all(
-        weighted.astype(jnp.bfloat16)[None], "lang", split_axis=2, concat_axis=0, tiled=True
-    )
+    own = weighted.astype(jnp.bfloat16)[None]
+    cells = jnp.split(own, lax.axis_size("lang"), axis=2)
+    got = lax.all_to_all(jnp.stack(cells), "lang", 0, 0)
+    pieces = jnp.concatenate(got, axis=0)
     shares = jnp.sum(pieces, axis=0, dtype=jnp.float32)
     grad_gate = shares[0].astype(jnp.bfloat16)
     grad_up = shares[1].astype(jnp.bfloat16)

time: 517 us -> 456 us (0.88)
  blocking collectives: 207 us -> 177 us
  local copies, waits for them, and re-layouts: 27 us -> 2.93 us
  other arithmetic: 36.2 us -> 29 us
    all_to_all x1, blocking collectives: 196 us -> 166 us  [body(): got = lax.all_to_all(jnp.stack(cells), 'lang', 0, 0)]
    convert_element_type x1 -> x0, local copies, waits for them, and re-layouts: 17.9 us -> none  [body(): weighted.astype(jnp.bfloat16)[None]]
  transfers between devices with their start and end apart: 2 -> 2, of which waited for: 1 -> 1; matrix products, arithmetic and copies ran while one was open for 18% -> 14% of each run, Pallas kernels for 0% -> 0%
where the time goes in v1:
time: 456 us; the launch traced here: 455 us
  blocking collectives  177 us (39%)
  waiting for transfers between devices  150 us (33%)
  matrix products  82.2 us (18%)
  other arithmetic  29 us (6%)
  between operations  14.2 us (3%)
    all_to_all x1, blocking collectives, body(): got = lax.all_to_all(jnp.stack(cells), 'lang', 0, 0)  166 us
    all_gather x1, waiting for transfers between devices, sent_together(): lax.all_gather(both, axis, axis=dim, tiled=True)  150 us
    dot_general x3, matrix products, contract_cols(): lax.dot_general(left, right, (((1,), (1,)), ((), ())), preferred_element_...  34 us
    dot_general x3, matrix products, contract_rows(): lax.dot_general(left, right, (((0,), (0,)), ((), ())), preferred_element_...  33.8 us
    all_to_all x1, blocking collectives, copy_for_each(): lax.all_to_all(jnp.broadcast_to(value[None], (length, *value.shape)), axi...  10.7 us
    convert_element_type x1, other arithmetic, body(): own = weighted.astype(jnp.bfloat16)[None]  9.59 us
  transfers between devices with their start and end apart: 2, of which 1 were waited for; matrix products, arithmetic and copies ran while one was open for 14% of the time, Pallas kernels for 0%

profile of v1, /device:TPU:0, one launch (start us, length us, event | category | flops | bytes accessed | tf_op | source)
XLA Modules:
  0.0 455.4 jit_solution(43791852890391510)
XLA Ops:
  7.2 0.0 all-gather.2.cloned.1.call-start
  7.2 2.7 pad_maximum_fusion
  10.0 0.0 all-gather.2.cloned.1.call-update
  10.0 0.0 reduce-scatter.2.cloned.1.call-start
  10.0 0.7 reduce.3
  10.7 0.4 convert_reduce_fusion
  11.1 150.3 %all-gather.2.cloned.1.call-done = bf16[2,768,8192]{2,1,0:T(8,128)(2,1)} async-done(((bf16[2,48,8192]{2,1,0:T(8,128)(2,1)}), bf16[2,768,8192]{2,1,0:T(8,128)(2,1)}) %all-gather.2.cloned.1.call-update) | async-done | bytes 25165840 | tf_op jit(solution)/shard_map/all_gather | solution.py:11
  161.4 0.0 copy-start.3
  161.4 7.8 %fusion.6 = f32[768,256]{1,0:T(8,128)S(1)} fusion(bf16[8192,256]{1,0:T(8,128)(2,1)} %param.9, bf16[2,768,8192]{2,1,0:T(8,128)(2,1)} %all-gather.2.cloned.1.call-done), kind=kOutput, calls=%fused_computation.11 | convolution fusion | flops 3221225472 | bytes 17563648 | tf_op jit(solution)/shard_map/dot_general | solution.py:49
  169.2 0.0 copy-done.3
  169.2 0.0 copy-start.4
  169.2 6.6 %fusion.7 = f32[768,256]{1,0:T(8,128)S(1)} fusion(bf16[8192,256]{1,0:T(8,128)(2,1)S(1)} %copy-done.3, bf16[2,768,8192]{2,1,0:T(8,128)(2,1)} %all-gather.2.cloned.1.call-done), kind=kOutput, calls=%fused_computation.12 | convolution fusion | flops 3221225472 | bytes 17563648 | tf_op jit(solution)/shard_map/dot_general | solution.py:50
  175.7 0.0 copy-done.4
  175.8 0.0 copy-start.2
  175.8 8.4 %multiply_convert_fusion.1 = (bf16[768,256]{1,0:T(8,128)(2,1)S(1)}, bf16[768,256]{1,0:T(8,128)(2,1)S(1)}) fusion(f32[768,256]{1,0:T(8,128)S(1)} %fusion.6, f32[768,256]{1,0:T(8,128)S(1)} %fusion.7, f32[768]{0:T(1024)S(1)} %broadcast_divide_fusion, bf16[256,8192]{1,0:T(8,128)(2,1)S(1)} %copy-done.4, bf16[2,768,8192]{2,1,0:T(8,128)(2,1)} %all-gather.2.cloned.1.call-done), kind=kOutput, calls=%fused_computation.33 | convolution fusion | flops 3223977984 | bytes 19139584 | tf_op jit(solution)/shard_map/dot_general | solution.py:36
  184.2 0.0 copy-done.2
  184.2 10.0 %fusion.22 = f32[768,8192]{1,0:T(8,128)} fusion(bf16[768,256]{1,0:T(8,128)(2,1)S(1)} %get-tuple-element.20, bf16[8192,256]{1,0:T(8,128)(2,1)S(1)} %copy-done.2), kind=kOutput, calls=%fused_computation.46 | convolution fusion | flops 3221225472 | bytes 29753344 | tf_op jit(solution)/shard_map/dot_general | solution.py:36
  194.2 15.6 %add_convert_fusion = bf16[768,8192]{1,0:T(8,128)(2,1)} fusion(f32[768,8192]{1,0:T(8,128)} %fusion.22, bf16[768,256]{1,0:T(8,128)(2,1)S(1)} %get-tuple-element.19, bf16[8192,256]{1,0:T(8,128)(2,1)} %param.10), kind=kOutput, calls=%fused_computation.4 | convolution fusion | flops 3233808384 | bytes 42336256 | tf_op jit(solution)/shard_map/dot_general | solution.py:36
  209.8 0.0 reduce-scatter.2.cloned.1.call-update
  209.8 7.3 %fusion.2 = f32[8192,256]{1,0:T(8,128)S(1)} fusion(bf16[2,768,8192]{2,1,0:T(8,128)(2,1)} %all-gather.2.cloned.1.call-done, f32[768,256]{1,0:T(8,128)S(1)} %fusion.7, f32[768]{0:T(1024)S(1)} %broadcast_divide_fusion, f32[768,256]{1,0:T(8,128)S(1)} %fusion.6), kind=kOutput, calls=%fused_computation.7 | convolution fusion | flops 3222601728 | bytes 22547456 | tf_op jit(solution)/shard_map/dot_general | solution.py:30
  217.1 0.0 copy-start
  217.1 11.2 %fusion.4 = f32[8192,256]{1,0:T(8,128)S(1)} fusion(bf16[768,256]{1,0:T(8,128)(2,1)S(1)} %get-tuple-element.19, bf16[2,768,8192]{2,1,0:T(8,128)(2,1)} %all-gather.2.cloned.1.call-done), kind=kOutput, calls=%fused_computation.9 | convolution fusion | flops 3221225472 | bytes 21364736 | tf_op jit(solution)/shard_map/dot_general | solution.py:30
  228.3 0.0 copy-start.1
  228.3 15.3 %fusion.5 = f32[8192,256]{1,0:T(8,128)} fusion(bf16[768,256]{1,0:T(8,128)(2,1)S(1)} %get-tuple-element.20, bf16[2,768,8192]{2,1,0:T(8,128)(2,1)} %all-gather.2.cloned.1.call-done), kind=kOutput, calls=%fused_computation.10 | convolution fusion | flops 3221225472 | bytes 21364736 | tf_op jit(solution)/shard_map/dot_general | solution.py:30
  243.7 0.0 copy-done
  243.7 0.0 copy-done.1
  243.7 8.9 %fusion.1 = f32[256]{0:T(256)S(1)} fusion(f32[1,8192,256]{2,1,0:T(8,128)S(1)} %bitcast.70, f32[1,8192,256]{2,1,0:T(8,128)S(1)} %bitcast.72, f32[1,8192,256]{2,1,0:T(8,128)} %bitcast.74), kind=kLoop, calls=%fused_computation.3 | loop fusion | flops 25165568 | bytes 25166848 | tf_op jit(solution)/shard_map/reduce_sum | solution.py:66
  252.6 10.7 %all_to_all.11 = f32[8,1,256]{2,1,0:T(1,128)S(1)} all-to-all(f32[8,1,256]{2,1,0:T(1,128)S(1)} %broadcast_in_dim.5), channel_id=1, replica_groups=mesh['lang'=8,'fsdp'=16] {'lang'}, dimensions={0} | all-to-all | bytes 16384 | tf_op jit(solution)/shard_map/all_to_all | solution.py:20
  263.4 9.6 %fusion = bf16[1,3,8192,256]{3,2,1,0:T(8,128)(2,1)S(1)} fusion(f32[1,1,8192,256]{3,2,1,0:T(8,128)} %bitcast.71, f32[1,1,8192,256]{3,2,1,0:T(8,128)} %bitcast.73, f32[1,1,8192,256]{3,2,1,0:T(8,128)} %bitcast.75, f32[256]{0:T(256)S(1)} %multiply_divide_fusion), kind=kLoop, calls=%fused_computation.1 | loop fusion | flops 25165824 | bytes 37749760 | tf_op jit(solution)/shard_map/convert_element_type | solution.py:70
  273.0 0.1 fusion.15
  273.1 0.1 fusion.14
  273.2 0.1 fusion.13
  273.3 0.1 fusion.12
  273.4 0.1 fusion.11
  273.5 0.1 fusion.10
  273.6 0.1 fusion.9
  273.8 0.1 fusion.8
  273.9 166.0 %all_to_all.12 = bf16[8,1,3,1024,256]{4,3,2,1,0:T(8,128)(2,1)} all-to-all(bf16[8,1,3,1024,256]{4,3,2,1,0:T(8,128)(2,1)S(1)} %fusion.8), channel_id=1, replica_groups=mesh['lang'=8,'fsdp'=16] {'lang'}, dimensions={0} | all-to-all | bytes 25165824 | tf_op jit(solution)/shard_map/all_to_all | solution.py:72
  439.9 6.6 %reduce.2 = bf16[3,1024,256]{2,1,0:T(8,128)(2,1)S(1)} reduce(bf16[8,1,3,1024,256]{4,3,2,1,0:T(8,128)(2,1)} %all_to_all.12, bf16[]{:T(256)} %constant.14), dimensions={0,1}, to_apply=%region_4.0.clone | reduce | flops 5505024 | bytes 14155778 | tf_op jit(solution)/shard_map/reduce_sum | solution.py:74
  446.5 1.1 slice_bitcast_fusion.18
  447.6 1.0 copy.13
  448.6 0.0 reduce-scatter.2.cloned.1.call-done
  (5 shorter events, 0.1 us)
Async XLA Ops:
  7.2 154.2 %all-gather.2.cloned.1.call-start = ((), (), s32[]{:S(2)}) async-start(), calls=%async_computation.3 | async-start | bytes 26738688 | tf_op jit(solution)/shard_map/all_gather | solution.py:11
  10.0 438.6 %reduce-scatter.2.cloned.1.call-start = ((), (), s32[]{:S(2)}) async-start(), calls=%async_computation.4 | async-start | bytes 13369344 | tf_op jit(solution)/shard_map/reduce_scatter | solution.py:78
  161.4 7.8 %copy-start.3 = (bf16[8192,256]{1,0:T(8,128)(2,1)S(1)}, bf16[8192,256]{1,0:T(8,128)(2,1)}, u32[]{:S(2)}) copy-start(bf16[8192,256]{1,0:T(8,128)(2,1)} %param.10) | copy-start | bytes 12582916
  169.2 6.6 %copy-start.4 = (bf16[256,8192]{1,0:T(8,128)(2,1)S(1)}, bf16[256,8192]{1,0:T(8,128)(2,1)}, u32[]{:S(2)}) copy-start(bf16[256,8192]{1,0:T(8,128)(2,1)} %param.11) | copy-start | bytes 12582916
  175.8 8.4 %copy-start.2 = (bf16[8192,256]{1,0:T(8,128)(2,1)S(1)}, bf16[8192,256]{1,0:T(8,128)(2,1)}, u32[]{:S(2)}) copy-start(bf16[8192,256]{1,0:T(8,128)(2,1)} %param.9) | copy-start | bytes 12582916
  217.1 26.6 %copy-start = (f32[8192,256]{1,0:T(8,128)}, f32[8192,256]{1,0:T(8,128)S(1)}, u32[]{:S(2)}) copy-start(f32[8192,256]{1,0:T(8,128)S(1)} %fusion.2) | copy-start | bytes 25165828
  228.3 15.3 %copy-start.1 = (f32[8192,256]{1,0:T(8,128)}, f32[8192,256]{1,0:T(8,128)S(1)}, u32[]{:S(2)}) copy-start(f32[8192,256]{1,0:T(8,128)S(1)} %fusion.4) | copy-start | bytes 25165828
Sparse Core Ops, SparseCore 0:
  10.4 150.9 all-gather.1
  210.0 146.3 reduce-scatter.1
